TPU v7x, 32 devices: a whole 2x2x4 slice. The times are simulated.
32 devices in a mesh: blk: 2 (over x), rows: 16 (over z, y, core).
Axes of the slice: x: 2, y: 2, z: 4, core: 2. Of those that a mesh axis runs over, the one named last changes fastest.
Arguments:
- features: bfloat16 [8192, 128], P(('blk', 'rows')), may hold values from -6 to 6
- labels: int32 [8192], P(('blk', 'rows')), may hold values from 0 to 6
- destination: int32 [8192, 1], P(('blk', 'rows')), may hold values from 0 to 15; in each aligned block of 256 rows (0 to 255, 256 to 511, ...) at most 32 rows name the same one
- centres: bfloat16 [8192, 128], P('blk'), may hold values from -6 to 6
- tri_inverse: float32 [8192, 8192], P('blk', 'rows'), may hold values from -1 to 2, as said below
- aux_inverse: float32 [8192, 8192], P('blk', 'rows'), may hold values from -1 to 2, as said below
Outputs:
- predictions: float32 [7, 16384], P(None, ('blk', 'rows'))
Inputs may be any that keep to these rules, and one draw needn't show every extreme that they name: `destination`: in each aligned block of 256 rows (the rows of one device) no value occurs more than 32 times, and some value occurs exactly 32 times. `tri_inverse`: zero below the diagonal, positive on it. `aux_inverse`: zero below the diagonal, positive on it.
All inputs are finite; a program needn't handle non-finite values.
Results may differ from a plain program's by a relative error of at most 0.0003.
Values may be sent and summed in bfloat16 or wider, within the bound.
A program may use at most 128 MiB of HBM per device.

v0:
```python
import functools

import jax
import jax.numpy as jnp
from jax import lax
from jax.experimental import pallas as pl
from jax.experimental.pallas import tpu as pltpu
from jax.sharding import PartitionSpec as P

CLASSES = 7
PAD = 8
MESH = pl.DeviceIdType.MESH
ridge_weight = 0.1
highest = lax.Precision.HIGHEST


def greet(peers, count):
    barrier = pltpu.get_barrier_semaphore()

    def hello(k, carry):
        pl.semaphore_signal(barrier, inc=1, device_id=peers(k), device_id_type=MESH)
        return carry

    lax.fori_loop(1, count, hello, 0)
    pl.semaphore_wait(barrier, count - 1)


def exchange(make, count, then):
    def send(k, carry):
        make(k).start()
        return carry

    def arrive(k, carry):
        make(k).wait_recv()
        return carry

    def left(k, carry):
        make(k).wait_send()
        return carry

    lax.fori_loop(1, count, send, 0)
    lax.fori_loop(1, count, arrive, 0)
    if then is not None:
        then()
    lax.fori_loop(1, count, left, 0)


def spot(index, chunk):
    return pl.ds(pl.multiple_of(index * chunk, chunk), chunk)


def add_parts(land):
    total = land[0]
    for index in range(1, land.shape[0]):
        total = total + land[index]
    return total


def spread_rows(nr, chunk, x_ref, land, s1, r1):
    b, r = lax.axis_index("blk"), lax.axis_index("rows")

    def make(k):
        other = lax.rem(r + k, nr)
        return pltpu.make_async_remote_copy(
            src_ref=x_ref.at[:, spot(other, chunk)],
            dst_ref=land.at[r],
            send_sem=s1.at[k],
            recv_sem=r1.at[k],
            device_id=(b, other),
            device_id_type=MESH,
        )

    land[r] = x_ref[:, spot(r, chunk)]
    return make


def plane_kernel(nb, nr, x_ref, o_ref, land, full, s1, r1, s2, r2):
    b, r = lax.axis_index("blk"), lax.axis_index("rows")
    chunk = land.shape[2]
    greet(lambda k: (b, lax.rem(r + k, nr)), nr)
    make = spread_rows(nr, chunk, x_ref, land, s1, r1)

    def add_up():
        full[:, spot(r, chunk)] = add_parts(land)

    exchange(make, nr, add_up)

    def gather(k):
        return pltpu.make_async_remote_copy(
            src_ref=full.at[:, spot(r, chunk)],
            dst_ref=full.at[:, spot(r, chunk)],
            send_sem=s2.at[k],
            recv_sem=r2.at[k],
            device_id=(b, lax.rem(r + k, nr)),
            device_id_type=MESH,
        )

    exchange(gather, nr, None)
    o_ref[...] = full[...]


def slice_kernel(nb, nr, x_ref, o_ref, land, mine, full, s1, r1, s2, r2):
    b, r = lax.axis_index("blk"), lax.axis_index("rows")
    me = b * nr + r
    chunk = land.shape[2]
    barrier = pltpu.get_barrier_semaphore()

    def hello(k, carry):
        pl.semaphore_signal(
            barrier, inc=1, device_id=(b, lax.rem(r + k, nr)), device_id_type=MESH
        )
        return carry

    lax.fori_loop(1, nr, hello, 0)
    for q in range(nb):
        source = r * nb + q

        @pl.when(source // nr != b)
        def _():
            pl.semaphore_signal(
                barrier,
                inc=1,
                device_id=(source // nr, lax.rem(source, nr)),
                device_id_type=MESH,
            )

    pl.semaphore_wait(barrier, nr - 1 + nb - 1)
    make = spread_rows(nr, chunk, x_ref, land, s1, r1)

    def add_up():
        mine[...] = add_parts(land)

    exchange(make, nr, add_up)
    taker, part = me // nb, lax.rem(me, nb)

    def deliver(q):
        return pltpu.make_async_remote_copy(
            src_ref=mine,
            dst_ref=full.at[:, spot(part, chunk)],
            send_sem=s2.at[q],
            recv_sem=r2.at[part],
            device_id=(q, taker),
            device_id_type=MESH,
        )

    def arrival(q):
        return pltpu.make_async_remote_copy(
            src_ref=mine,
            dst_ref=full.at[:, spot(q, chunk)],
            send_sem=s2.at[q],
            recv_sem=r2.at[q],
            device_id=(b, r),
            device_id_type=MESH,
        )

    for q in range(nb):
        own = q * nr + taker == me

        @pl.when(jnp.logical_not(own))
        def _():
            deliver(q).start()

        @pl.when(own)
        def _():
            full[:, spot(part, chunk)] = mine[...]

    for q in range(nb):

        @pl.when(r * nb + q != me)
        def _():
            arrival(q).wait_recv()

    for q in range(nb):

        @pl.when(q * nr + taker != me)
        def _():
            deliver(q).wait_send()

    o_ref[...] = full[...]


def turn_kernel(nb, nr, x_ref, add_ref, o_ref, land, mine, full, s1, r1, s2, r2):
    b, r = lax.axis_index("blk"), lax.axis_index("rows")
    me = b * nr + r
    chunk = land.shape[2]
    place = r * nb + b
    plane, part = place // nr, lax.rem(place, nr)
    barrier = pltpu.get_barrier_semaphore()
    for k in range(1, nb):
        pl.semaphore_signal(
            barrier, inc=1, device_id=(lax.rem(b + k, nb), r), device_id_type=MESH
        )

    def hello(p, carry):
        whose = b * nr + p
        side, line = lax.rem(whose, nb), whose // nb

        @pl.when(side * nr + line != me)
        def _():
            pl.semaphore_signal(barrier, inc=1, device_id=(side, line), device_id_type=MESH)

        return carry

    lax.fori_loop(0, nr, hello, 0)
    pl.semaphore_wait(barrier, nb - 1 + nr - (plane == b).astype(jnp.int32))

    def make(k):
        other = lax.rem(b + k, nb)
        return pltpu.make_async_remote_copy(
            src_ref=x_ref.at[:, spot(other, chunk)],
            dst_ref=land.at[b],
            send_sem=s1.at[k],
            recv_sem=r1.at[k],
            device_id=(other, r),
            device_id_type=MESH,
        )

    land[b] = x_ref[:, spot(b, chunk)]

    def add_up():
        mine[...] = add_parts(land) + add_ref[:, spot(b, chunk)]

    exchange(make, nb, add_up)

    def deliver(k):
        other = lax.rem(r + k, nr)
        return other, pltpu.make_async_remote_copy(
            src_ref=mine,
            dst_ref=full.at[:, spot(part, chunk)],
            send_sem=s2.at[k],
            recv_sem=r2.at[part],
            device_id=(plane, other),
            device_id_type=MESH,
        )

    def arrival(p):
        return pltpu.make_async_remote_copy(
            src_ref=mine,
            dst_ref=full.at[:, spot(p, chunk)],
            send_sem=s2.at[p],
            recv_sem=r2.at[p],
            device_id=(b, r),
            device_id_type=MESH,
        )

    def start(k, carry):
        deliver(k)[1].start()
        return carry

    def arrive(p, carry):
        whose = b * nr + p

        @pl.when(lax.rem(whose, nb) * nr + whose // nb != me)
        def _():
            arrival(p).wait_recv()

        return carry

    def left(k, carry):
        deliver(k)[1].wait_send()
        return carry

    @pl.when(plane != b)
    def _():
        deliver(0)[1].start()

    lax.fori_loop(1, nr, start, 0)

    @pl.when(plane == b)
    def _():
        full[:, spot(part, chunk)] = mine[...]

    lax.fori_loop(0, nr, arrive, 0)

    @pl.when(plane != b)
    def _():
        deliver(0)[1].wait_send()

    lax.fori_loop(1, nr, left, 0)
    o_ref[...] = full[...]


def swap_kernel(kind, nb, nr, x_ref, o_ref, land, s1, r1):
    b, r = lax.axis_index("blk"), lax.axis_index("rows")
    across = kind in ("pair", "images", "share")
    parts, own = (nb, b) if across else (nr, r)

    def device(k):
        other = lax.rem(own + k, parts)
        return (other, r) if across else (b, other)

    greet(device, parts)

    def make(k):
        source = x_ref.at[lax.rem(own + k, parts)] if kind == "move" else x_ref
        return pltpu.make_async_remote_copy(
            src_ref=source,
            dst_ref=land.at[own],
            send_sem=s1.at[k],
            recv_sem=r1.at[k],
            device_id=device(k),
            device_id_type=MESH,
        )

    land[own] = x_ref[own] if kind == "move" else x_ref[...]

    def finish():
        o_ref[...] = land[...] if kind in ("move", "share") else add_parts(land)

    exchange(make, parts, finish)


KINDS = ("plane", "slice", "turn", "pair", "images", "share", "total", "move")


def call(kind, body, nb, nr, shape, dtype, scratch, *operands):
    whole = pl.BlockSpec(memory_space=pltpu.VMEM)
    return pl.pallas_call(
        functools.partial(body, nb, nr),
        out_shape=jax.ShapeDtypeStruct(shape, dtype),
        in_specs=[whole] * len(operands),
        out_specs=whole,
        scratch_shapes=scratch,
        compiler_params=pltpu.CompilerParams(
            collective_id=KINDS.index(kind), has_side_effects=True
        ),
    )(*operands)


def plain(nb, nr):
    return nb * nr > 64 or nb != 2


dma = pltpu.SemaphoreType.DMA


def float_buffer(*shape):
    return pltpu.VMEM(shape, jnp.float32)


def plane_sum(nb, nr, x):
    if plain(nb, nr):
        return lax.psum(x, "rows")
    width = x.shape[1]
    scratch = [float_buffer(nr, PAD, width // nr), float_buffer(PAD, width)] + [dma((nr,))] * 4
    return call("plane", plane_kernel, nb, nr, x.shape, jnp.float32, scratch, x)


def slice_sum(nb, nr, x):
    size = x.shape[1] * nb // nr
    if plain(nb, nr):
        full = lax.all_gather(lax.psum(x, "rows"), "blk", axis=1, tiled=True)
        return lax.dynamic_slice_in_dim(full, lax.axis_index("rows") * size, size, 1)
    chunk = x.shape[1] // nr
    scratch = [
        float_buffer(nr, PAD, chunk),
        float_buffer(PAD, chunk),
        float_buffer(PAD, size),
        dma((nr,)),
        dma((nr,)),
        dma((nb,)),
        dma((nb,)),
    ]
    return call("slice", slice_kernel, nb, nr, (PAD, size), jnp.float32, scratch, x)


def turn_sum(nb, nr, x, add):
    width = x.shape[1] * nr // nb
    if plain(nb, nr):
        full = lax.all_gather(lax.psum(x, "blk") + add, "rows", axis=1, tiled=True)
        return lax.dynamic_slice_in_dim(full, lax.axis_index("blk") * width, width, 1)
    chunk = x.shape[1] // nb
    scratch = [
        float_buffer(nb, PAD, chunk),
        float_buffer(PAD, chunk),
        float_buffer(PAD, width),
        dma((nb,)),
        dma((nb,)),
        dma((nr,)),
        dma((nr,)),
    ]
    return call("turn", turn_kernel, nb, nr, (PAD, width), jnp.float32, scratch, x, add)


def swapped(kind, nb, nr, x):
    if plain(nb, nr):
        if kind == "total":
            return lax.psum(x, "rows")
        if kind == "move":
            return lax.all_to_all(x, "rows", split_axis=0, concat_axis=0, tiled=True)
        if kind == "share":
            return lax.all_gather(x, "blk", axis=0)
        return lax.psum(x, "blk")
    parts = nr if kind in ("total", "move") else nb
    land = x.shape if kind == "move" else (parts,) + x.shape
    shape = land if kind == "share" else x.shape
    scratch = [pltpu.VMEM(land, x.dtype), dma((parts,)), dma((parts,))]
    return call(kind, functools.partial(swap_kernel, kind), nb, nr, shape, x.dtype, scratch, x)


def three_parts(x):
    high = x.astype(jnp.bfloat16).astype(jnp.float32)
    rest = x - high
    mid = rest.astype(jnp.bfloat16).astype(jnp.float32)
    return high, mid, rest - mid


def exact_product(dims, vector, block):
    stacked = jnp.concatenate(three_parts(vector), axis=0).astype(jnp.bfloat16)
    total = None
    for part in reversed(three_parts(block)):
        product = lax.dot_general(
            stacked, part.astype(jnp.bfloat16), dims, preferred_element_type=jnp.float32
        )
        product = product[2 * PAD :] + product[PAD : 2 * PAD] + product[:PAD]
        total = product if total is None else total + product
    return total


def forward_kernel(u_ref, block_ref, o_ref):
    o_ref[...] = exact_product((((1,), (1,)), ((), ())), u_ref[...], block_ref[...])


def backward_kernel(u_ref, block_ref, o_ref):
    product = exact_product((((1,), (0,)), ((), ())), u_ref[...], block_ref[...])

    @pl.when(pl.program_id(0) == 0)
    def _():
        o_ref[...] = product

    @pl.when(pl.program_id(0) > 0)
    def _():
        o_ref[...] += product


STEP = 512


def factor_forward(block, vector):
    rows, cols = block.shape
    return pl.pallas_call(
        forward_kernel,
        grid=(rows // STEP,),
        in_specs=[
            pl.BlockSpec((PAD, cols), lambda i: (0, 0)),
            pl.BlockSpec((STEP, cols), lambda i: (i, 0)),
        ],
        out_specs=pl.BlockSpec((PAD, STEP), lambda i: (0, i)),
        out_shape=jax.ShapeDtypeStruct((PAD, rows), jnp.float32),
    )(vector, block)


def factor_backward(block, vector):
    rows, cols = block.shape
    return pl.pallas_call(
        backward_kernel,
        grid=(rows // STEP,),
        in_specs=[
            pl.BlockSpec((PAD, STEP), lambda i: (0, i)),
            pl.BlockSpec((STEP, cols), lambda i: (i, 0)),
        ],
        out_specs=pl.BlockSpec((PAD, cols), lambda i: (0, 0)),
        out_shape=jax.ShapeDtypeStruct((PAD, cols), jnp.float32),
    )(vector, block)


def square_norms(rows_x):
    return jnp.einsum("nd,nd->n", rows_x, rows_x, preferred_element_type=jnp.float32)


def to_low(values):
    return lax.reduce_precision(values, 8, 7).astype(jnp.bfloat16)


def with_scalars(vector, scalars):
    return vector + jnp.pad(scalars[None, :], ((PAD - 1, 0), (0, vector.shape[1] - PAD)))


def on_device(nb, nr, features, labels, destination, centres, tri_inverse, aux_inverse):
    own_rows, width = features.shape
    capacity = max(2, 2 * own_rows // nr)
    scale = 2.0 / width
    count_all = float(own_rows * nb * nr)
    b = lax.axis_index("blk")
    class_rows = jnp.arange(PAD, dtype=jnp.int32)[:, None]
    real = class_rows < CLASSES

    tags = jnp.pad(labels.astype(jnp.bfloat16), (0, -own_rows % (16 * width)))
    tags = tags.reshape(-1, width)
    shared = swapped("share", nb, nr, jnp.concatenate([features, tags], axis=0))
    rows_x = shared[:, :own_rows].reshape(nb * own_rows, width)
    tags = shared[:, own_rows:].reshape(nb, -1)[:, :own_rows].reshape(nb * own_rows)
    centre_norm = square_norms(centres)
    rows_norm = square_norms(rows_x)
    inner = lax.dot_general(
        rows_x, centres, (((1,), (1,)), ((), ())), preferred_element_type=jnp.float32
    )
    kmat = jnp.exp(-(rows_norm[:, None] + centre_norm[None, :] - 2.0 * inner) * scale).astype(
        jnp.bfloat16
    )
    hits = tags.astype(jnp.float32)[None, :] == class_rows.astype(jnp.float32)
    targets = jnp.where(real, jnp.where(hits, 1.0, -1.0), 0.0).astype(jnp.bfloat16)

    def clean(vector):
        return jnp.where(real, vector, 0.0)

    def onto_rows(low):
        return lax.dot_general(
            low, kmat, (((1,), (1,)), ((), ())), preferred_element_type=jnp.float32
        )

    def images(second):
        high = to_low(second)
        rest = second - high.astype(jnp.float32)
        mid = to_low(rest)
        low = to_low(rest - mid.astype(jnp.float32))
        three = onto_rows(jnp.concatenate([high, mid, low], axis=0))
        both = jnp.concatenate([three[:PAD], three[PAD : 2 * PAD] + three[2 * PAD :]], axis=0)
        both = swapped("images", nb, nr, both)
        image = to_low(both[:PAD])
        exact = both[:PAD] + both[PAD:]
        curve = jnp.sum(image.astype(jnp.float32) * exact, axis=1) / count_all
        return image, curve

    def ratio(above, below):
        return jnp.where(real, (above / below)[:, None], 0.0)

    def normal(vector):
        return jnp.sum(vector * vector, axis=1)

    start = plane_sum(nb, nr, jnp.dot(targets, kmat, preferred_element_type=jnp.float32) / count_all)
    start = factor_backward(tri_inverse, start)
    start = turn_sum(nb, nr, start, jnp.zeros_like(start))
    rhs = swapped("pair", nb, nr, factor_backward(aux_inverse, start))
    first = slice_sum(nb, nr, factor_forward(aux_inverse, rhs))
    joined = plane_sum(nb, nr, with_scalars(factor_forward(tri_inverse, first), normal(rhs)))
    norm_first = joined[PAD - 1, :PAD]
    second = clean(joined)
    image, curve = images(second)
    curve = curve + ridge_weight * normal(first)
    gram = jnp.dot(image, kmat, preferred_element_type=jnp.float32) / count_all
    joined = plane_sum(nb, nr, with_scalars(gram, curve))
    step_first = ratio(norm_first, joined[PAD - 1, :PAD])
    third = turn_sum(nb, nr, factor_backward(tri_inverse, clean(joined)), ridge_weight * first)
    turned = swapped("pair", nb, nr, factor_backward(aux_inverse, third))
    residual = rhs - step_first * turned
    first_next = slice_sum(nb, nr, factor_forward(aux_inverse, residual))
    joined = plane_sum(nb, nr, with_scalars(factor_forward(tri_inverse, first_next), normal(residual)))
    norm_next = joined[PAD - 1, :PAD]
    turn_weight = ratio(norm_next, norm_first)
    first_next = first_next + turn_weight * first
    second_next = clean(joined) + turn_weight * second
    image, curve = images(second_next)
    curve = curve + ridge_weight * normal(first_next)
    curve = swapped("total", nb, nr, jnp.pad(curve[:, None], ((0, 0), (0, 127))))[:, 0]
    step_next = ratio(norm_next, curve)
    coefficients = step_first * second + step_next * second_next
    scores = swapped("pair", nb, nr, onto_rows(to_low(coefficients)))
    scores = lax.dynamic_slice_in_dim(scores, b * own_rows, own_rows, 1)

    target = destination[:, 0]
    row_ids = jnp.arange(own_rows, dtype=jnp.int32)
    same = (target[:, None] == target[None, :]) & (row_ids[None, :] < row_ids[:, None])
    before = jnp.sum(same.astype(jnp.int32), axis=1)
    slots = nr * capacity
    spread = (
        (target * capacity + before)[:, None] == jnp.arange(slots, dtype=jnp.int32)[None, :]
    ).astype(jnp.float32)
    placed = jnp.dot(scores, spread, precision=highest, preferred_element_type=jnp.float32)
    placed = placed.reshape(PAD, nr, capacity).transpose(1, 0, 2)
    lanes = -capacity % 128
    moved = swapped("move", nb, nr, jnp.pad(placed, ((0, 0), (0, 0), (0, lanes))))
    moved = moved[:, :CLASSES, :capacity]
    return moved.transpose(1, 0, 2).reshape(CLASSES, slots)


def solution(mesh):
    return jax.shard_map(
        functools.partial(on_device, mesh.shape["blk"], mesh.shape["rows"]),
        mesh=mesh,
        in_specs=(
            P(("blk", "rows"), None),
            P(("blk", "rows")),
            P(("blk", "rows"), None),
            P("blk", None),
            P("blk", "rows"),
            P("blk", "rows"),
        ),
        out_specs=P(None, ("blk", "rows")),
        check_vma=False,
    )
```

profile of v0, /device:TPU:0, one launch (start us, length us, event | category | flops | bytes accessed | tf_op | source)
XLA Modules:
  0.0 275.0 jit_solution(11310804607525308751)
XLA Ops:
  0.0 0.9 convert_reduce_fusion
  0.9 0.7 multiply_add_fusion.1
  1.6 0.7 convert_element_type.86
  2.3 1.5 pad_maximum_fusion.x_ref
  3.8 6.8 %shard_map.64 = bf16[2,272,128]{2,1,0:T(8,128)(2,1)} custom-call(bf16[272,128]{1,0:T(8,128)(2,1)} %pad_maximum_fusion.x_ref), custom_call_target="tpu_custom_call" | custom-call | tf_op jit(solution)/shard_map/pallas_call | solution.py:318
  10.6 0.9 slice.58
  11.5 1.8 fusion.1
  13.4 0.2 fusion.3
  13.5 3.6 %exponential_convert_fusion = bf16[512,4096]{1,0:T(8,128)(2,1)S(1)} fusion(bf16[512,128]{1,0:T(8,128)(2,1)S(1)} %bitcast.39, bf16[4096,128]{1,0:T(8,128)(2,1)} %param.9, f32[4096]{0:T(1024)S(1)} %fusion.1, f32[512]{0:T(512)S(1)} %fusion.3), kind=kOutput, calls=%fused_computation | convolution fusion | flops 549453824 | bytes 5392384 | tf_op jit(solution)/shard_map/dot_general | solution.py:495
  17.1 0.7 slice_bitcast_fusion.1
  17.9 1.1 copy-done
  19.0 1.3 convolution_multiply_fusion.1.x_ref
  20.4 17.0 %shard_map.65.u_ref = f32[8,4096]{1,0:T(8,128)} custom-call(f32[8,4096]{1,0:T(8,128)} %convolution_multiply_fusion.1.x_ref), custom_call_target="tpu_custom_call" | custom-call | tf_op jit(solution)/shard_map/pallas_call | solution.py:318
  37.3 8.3 %shard_map.66.x_ref = f32[8,512]{1,0:T(8,128)} custom-call(f32[8,4096]{1,0:T(8,128)} %shard_map.65.u_ref, f32[4096,512]{1,0:T(8,128)} %block_ref.15), custom_call_target="tpu_custom_call" | custom-call | tf_op jit(solution)/shard_map/pallas_call | solution.py:455
  45.6 0.6 broadcast_in_dim.75.add_ref
  46.2 10.4 %shard_map.67.u_ref = f32[8,4096]{1,0:T(8,128)} custom-call(f32[8,512]{1,0:T(8,128)} %shard_map.66.x_ref, f32[8,512]{1,0:T(8,128)} %broadcast_in_dim.75.add_ref), custom_call_target="tpu_custom_call" | custom-call | tf_op jit(solution)/shard_map/pallas_call | solution.py:318
  56.6 8.3 %shard_map.68.x_ref = f32[8,512]{1,0:T(8,128)} custom-call(f32[8,4096]{1,0:T(8,128)} %shard_map.67.u_ref, f32[4096,512]{1,0:T(8,128)} %block_ref.14), custom_call_target="tpu_custom_call" | custom-call | tf_op jit(solution)/shard_map/pallas_call | solution.py:455
  64.9 5.5 %shard_map.69.u_ref = f32[8,512]{1,0:T(8,128)} custom-call(f32[8,512]{1,0:T(8,128)} %shard_map.68.x_ref), custom_call_target="tpu_custom_call" | custom-call | tf_op jit(solution)/shard_map/pallas_call | solution.py:318
  70.4 8.8 %shard_map.70.x_ref = f32[8,4096]{1,0:T(8,128)} custom-call(f32[8,512]{1,0:T(8,128)} %shard_map.69.u_ref, f32[4096,512]{1,0:T(8,128)} %block_ref.14), custom_call_target="tpu_custom_call" | custom-call | tf_op jit(solution)/shard_map/pallas_call | solution.py:441
  79.2 10.5 %shard_map.71.u_ref = f32[8,512]{1,0:T(8,128)} custom-call(f32[8,4096]{1,0:T(8,128)} %shard_map.70.x_ref), custom_call_target="tpu_custom_call" | custom-call | tf_op jit(solution)/shard_map/pallas_call | solution.py:318
  89.7 8.8 %shard_map.72 = f32[8,4096]{1,0:T(8,128)} custom-call(f32[8,512]{1,0:T(8,128)} %shard_map.71.u_ref, f32[4096,512]{1,0:T(8,128)} %block_ref.15), custom_call_target="tpu_custom_call" | custom-call | tf_op jit(solution)/shard_map/pallas_call | solution.py:441
  98.6 0.1 multiply_reduce_fusion.5
  98.7 1.6 pad_add_fusion.1.x_ref
  100.2 17.3 %shard_map.73 = f32[8,4096]{1,0:T(8,128)} custom-call(f32[8,4096]{1,0:T(8,128)} %pad_add_fusion.1.x_ref), custom_call_target="tpu_custom_call" | custom-call | tf_op jit(solution)/shard_map/pallas_call | solution.py:318
  117.6 1.0 reduce-precision_convert_fusion.6
  118.6 3.4 %fusion.6 = f32[24,512]{1,0:T(8,128)S(1)} fusion(bf16[512,4096]{1,0:T(8,128)(2,1)} %copy-done, bf16[8,4096]{1,0:T(8,128)(2,1)S(1)} %get-tuple-element.10, bf16[8,4096]{1,0:T(8,128)(2,1)S(1)} %get-tuple-element.11, bf16[8,4096]{1,0:T(8,128)(2,1)S(1)} %get-tuple-element.9), kind=kOutput, calls=%fused_computation.14 | convolution fusion | flops 101253120 | bytes 4440064 | tf_op jit(solution)/shard_map/dot_general | solution.py:508
  122.0 0.6 pad_maximum_fusion.1.x_ref
  122.6 5.3 %shard_map.74 = f32[16,512]{1,0:T(8,128)} custom-call(f32[16,512]{1,0:T(8,128)} %pad_maximum_fusion.1.x_ref), custom_call_target="tpu_custom_call" | custom-call | tf_op jit(solution)/shard_map/pallas_call | solution.py:318
  127.9 1.5 broadcast_multiply_fusion
  129.4 3.5 %fusion.x_ref = f32[8,4096]{1,0:T(8,128)} fusion(bf16[512,4096]{1,0:T(8,128)(2,1)} %copy-done, f32[1,8]{1,0:T(1,128)S(1)} %add_bitcast_fusion.1, f32[16,512]{1,0:T(8,128)} %shard_map.74), kind=kOutput, calls=%fused_computation.2 | convolution fusion | flops 33628160 | bytes 4341792 | tf_op jit(solution)/shard_map/dot_general | solution.py:541
  132.9 15.0 %shard_map.75 = f32[8,4096]{1,0:T(8,128)} custom-call(f32[8,4096]{1,0:T(8,128)} %fusion.x_ref), custom_call_target="tpu_custom_call" | custom-call | tf_op jit(solution)/shard_map/pallas_call | solution.py:318
  148.0 1.6 broadcast_select_fusion.u_ref
  149.6 8.3 %shard_map.76.x_ref = f32[8,512]{1,0:T(8,128)} custom-call(f32[8,4096]{1,0:T(8,128)} %broadcast_select_fusion.u_ref, f32[4096,512]{1,0:T(8,128)} %block_ref.15), custom_call_target="tpu_custom_call" | custom-call | tf_op jit(solution)/shard_map/pallas_call | solution.py:455
  157.9 10.4 %shard_map.77.u_ref = f32[8,4096]{1,0:T(8,128)} custom-call(f32[8,512]{1,0:T(8,128)} %shard_map.76.x_ref, f32[8,512]{1,0:T(8,128)} %get-tuple-element.18.add_ref), custom_call_target="tpu_custom_call" | custom-call | tf_op jit(solution)/shard_map/pallas_call | solution.py:318
  168.3 8.3 %shard_map.78.x_ref = f32[8,512]{1,0:T(8,128)} custom-call(f32[8,4096]{1,0:T(8,128)} %shard_map.77.u_ref, f32[4096,512]{1,0:T(8,128)} %block_ref.14), custom_call_target="tpu_custom_call" | custom-call | tf_op jit(solution)/shard_map/pallas_call | solution.py:455
  176.6 5.6 %shard_map.79 = f32[8,512]{1,0:T(8,128)} custom-call(f32[8,512]{1,0:T(8,128)} %shard_map.78.x_ref), custom_call_target="tpu_custom_call" | custom-call | tf_op jit(solution)/shard_map/pallas_call | solution.py:318
  182.2 0.7 bitcast_select_fusion.1
  182.8 1.5 multiply_reduce_fusion.2
  184.4 8.8 %shard_map.80.x_ref = f32[8,4096]{1,0:T(8,128)} custom-call(f32[8,512]{1,0:T(8,128)} %get-tuple-element.8.u_ref, f32[4096,512]{1,0:T(8,128)} %block_ref.14), custom_call_target="tpu_custom_call" | custom-call | tf_op jit(solution)/shard_map/pallas_call | solution.py:441
  193.2 10.9 %shard_map.81.u_ref = f32[8,512]{1,0:T(8,128)} custom-call(f32[8,4096]{1,0:T(8,128)} %shard_map.80.x_ref), custom_call_target="tpu_custom_call" | custom-call | tf_op jit(solution)/shard_map/pallas_call | solution.py:318
  204.0 8.9 %shard_map.82 = f32[8,4096]{1,0:T(8,128)} custom-call(f32[8,512]{1,0:T(8,128)} %shard_map.81.u_ref, f32[4096,512]{1,0:T(8,128)} %block_ref.15), custom_call_target="tpu_custom_call" | custom-call | tf_op jit(solution)/shard_map/pallas_call | solution.py:441
  213.0 1.5 pad_add_fusion.x_ref
  214.5 17.0 %shard_map.83 = f32[8,4096]{1,0:T(8,128)} custom-call(f32[8,4096]{1,0:T(8,128)} %pad_add_fusion.x_ref), custom_call_target="tpu_custom_call" | custom-call | tf_op jit(solution)/shard_map/pallas_call | solution.py:318
  231.6 0.7 bitcast_select_fusion
  232.3 1.0 reduce-precision_convert_fusion.3
  233.3 0.7 slice_bitcast_fusion.2
  234.0 0.1 copy.14
  234.0 0.2 multiply_reduce_fusion
  234.3 3.4 %fusion.12 = f32[24,512]{1,0:T(8,128)S(1)} fusion(bf16[512,4096]{1,0:T(8,128)(2,1)} %copy-done, bf16[8,4096]{1,0:T(8,128)(2,1)S(1)} %get-tuple-element.13, bf16[8,4096]{1,0:T(8,128)(2,1)S(1)} %get-tuple-element.12, bf16[8,4096]{1,0:T(8,128)(2,1)S(1)} %get-tuple-element.5), kind=kOutput, calls=%fused_computation.20 | convolution fusion | flops 101253120 | bytes 4440064 | tf_op jit(solution)/shard_map/dot_general | solution.py:508
  237.7 0.6 pad_maximum_fusion.2.x_ref
  238.3 5.3 %shard_map.84 = f32[16,512]{1,0:T(8,128)} custom-call(f32[16,512]{1,0:T(8,128)} %pad_maximum_fusion.2.x_ref), custom_call_target="tpu_custom_call" | custom-call | tf_op jit(solution)/shard_map/pallas_call | solution.py:318
  243.6 0.9 multiply_reduce_fusion.1
  244.5 0.1 copy.13
  244.6 0.6 pad.26.x_ref
  245.2 8.0 %shard_map.85 = f32[8,128]{1,0:T(8,128)} custom-call(f32[8,128]{1,0:T(8,128)} %pad.26.x_ref), custom_call_target="tpu_custom_call" | custom-call | tf_op jit(solution)/shard_map/pallas_call | solution.py:318
  253.2 0.8 select_reduce_fusion
  254.0 4.0 %fusion.18.x_ref = f32[8,512]{1,0:T(8,128)} fusion(bf16[512,4096]{1,0:T(8,128)(2,1)} %copy-done, f32[8,4096]{1,0:T(8,128)S(1)} %get-tuple-element.6, f32[8,4096]{1,0:T(8,128)S(1)} %copy-done.1, f32[8]{0:T(128)S(1)} %select_reduce_fusion, f32[8]{0:T(128)S(1)} %bitcast_select_fusion.1, pred[8]{0:T(512)(128)(4,1)S(1)} %iota_compare_fusion.4), kind=kOutput, calls=%fused_computation.39 | convolution fusion | flops 33751040 | bytes 4472904 | tf_op jit(solution)/shard_map/dot_general | solution.py:508
  258.0 5.1 %shard_map.86 = f32[8,512]{1,0:T(8,128)} custom-call(f32[8,512]{1,0:T(8,128)} %fusion.18.x_ref), custom_call_target="tpu_custom_call" | custom-call | tf_op jit(solution)/shard_map/pallas_call | solution.py:318
  263.1 1.0 fusion.2
  264.1 0.1 reshape.116
  264.2 0.6 pad.27.x_ref
  264.9 8.6 %shard_map.87 = f32[16,8,128]{2,1,0:T(8,128)} custom-call(f32[16,8,128]{2,1,0:T(8,128)} %pad.27.x_ref), custom_call_target="tpu_custom_call" | custom-call | tf_op jit(solution)/shard_map/pallas_call | solution.py:318
  273.4 0.8 slice_bitcast_fusion
  274.3 0.7 reshape.117
  (22 shorter events, 0.2 us)
Async XLA Ops:
  17.1 1.9 copy-start
  89.7 8.8 %copy-start.2 = (f32[8,512]{1,0:T(8,128)S(1)}, f32[8,512]{1,0:T(8,128)}, u32[]{:S(2)}) copy-start(f32[8,512]{1,0:T(8,128)} %shard_map.69.u_ref) | copy-start | bytes 49156
  98.6 29.4 %copy-start.3 = (f32[8,512]{1,0:T(8,128)S(1)}, f32[8,512]{1,0:T(8,128)}, u32[]{:S(2)}) copy-start(f32[8,512]{1,0:T(8,128)} %shard_map.71.u_ref) | copy-start | bytes 49156
  168.3 13.9 %copy-start.1 = (f32[8,4096]{1,0:T(8,128)S(1)}, f32[8,4096]{1,0:T(8,128)}, u32[]{:S(2)}) copy-start(f32[8,4096]{1,0:T(8,128)} %shard_map.73) | copy-start | bytes 393220
  204.0 30.0 %copy-start.4 = (f32[8,512]{1,0:T(8,128)S(1)}, f32[8,512]{1,0:T(8,128)}, u32[]{:S(2)}) copy-start(f32[8,512]{1,0:T(8,128)} %shard_map.81.u_ref) | copy-start | bytes 49156
where the time goes:
time: 278 us; the launch traced here: 275 us
  Pallas kernels  227 us (82%)
  matrix products  20.2 us (7%)
  other arithmetic  20.1 us (7%)
  local copies, waits for them, and re-layouts  7.17 us (3%)
    pallas_call x16, Pallas kernels, call(): pl.pallas_call(functools.partial(body, nb, nr), out_shape=jax.ShapeDtypeS...  159 us
    pallas_call x4, Pallas kernels, factor_forward(): pl.pallas_call(forward_kernel, grid=(rows // STEP,), in_specs=[pl.BlockSp...  35.4 us
    pallas_call x4, Pallas kernels, factor_backward(): pl.pallas_call(backward_kernel, grid=(rows // STEP,), in_specs=[pl.BlockS...  33.1 us
    dot_general x3, matrix products, onto_rows(): lax.dot_general(low, kmat, (((1,), (1,)), ((), ())), preferred_element_ty...  10.7 us

commit v1 on v0

--- a/solution.py
+++ b/solution.py
@@ -468,6 +468,93 @@
     return jnp.einsum("nd,nd->n", rows_x, rows_x, preferred_element_type=jnp.float32)
 
 
+def factor_loop(forward, vector_ref, clean, block, p_ref):
+    steps = block.shape[0] // STEP
+    lines = lax.broadcasted_iota(jnp.int32, (PAD, STEP), 0)
+
+    def visit(i, carry):
+        piece = block[spot(i, STEP), :]
+        if forward:
+            p_ref[:, spot(i, STEP)] = exact_product(
+                (((1,), (1,)), ((), ())), vector_ref[...], piece
+            )
+            return carry
+        ours = vector_ref[:, spot(i, STEP)]
+        if clean:
+            ours = jnp.where(lines < CLASSES, ours, 0.0)
+        p_ref[...] += exact_product((((1,), (0,)), ((), ())), ours, piece)
+        return carry
+
+    if not forward:
+        p_ref[...] = jnp.zeros_like(p_ref)
+    lax.fori_loop(0, steps, visit, 0)
+
+
+def joint_kernel(kind, nb, nr, *refs):
+    inputs = {"plane": 1, "slice": 1, "turn": 2, "pair": 3}[kind]
+    block_ref, o_ref, p_ref, block, block_sem = refs[inputs : inputs + 5]
+    rest = refs[inputs + 5 :]
+    load = pltpu.make_async_copy(block_ref, block, block_sem)
+    load.start()
+    if kind == "plane":
+        plane_kernel(nb, nr, refs[0], o_ref, *rest)
+    elif kind == "slice":
+        slice_kernel(nb, nr, refs[0], o_ref, *rest)
+    elif kind == "turn":
+        turn_kernel(nb, nr, refs[0], refs[1], o_ref, *rest)
+    else:
+        swap_kernel("pair", nb, nr, refs[0], o_ref, *rest)
+        o_ref[...] = refs[1][...] + refs[2][...] * o_ref[...]
+    load.wait()
+    factor_loop(kind in ("slice", "pair"), o_ref, kind == "plane", block, p_ref)
+
+
+def joint_sum(kind, nb, nr, block, *operands):
+    rows, cols = block.shape
+    x = operands[0]
+    forward = kind in ("slice", "pair")
+    if plain(nb, nr):
+        if kind == "plane":
+            out = plane_sum(nb, nr, x)
+            lines = jnp.arange(PAD, dtype=jnp.int32)[:, None]
+            return out, factor_backward(block, jnp.where(lines < CLASSES, out, 0.0))
+        if kind == "turn":
+            out = turn_sum(nb, nr, *operands)
+            return out, factor_backward(block, out)
+        if kind == "slice":
+            out = slice_sum(nb, nr, x)
+        else:
+            out = operands[1] + operands[2] * swapped("pair", nb, nr, x)
+        return out, factor_forward(block, out)
+    size, wide = (cols, rows) if forward else (rows, cols)
+    if kind == "plane":
+        chunk = rows // nr
+        scratch = [float_buffer(nr, PAD, chunk), float_buffer(PAD, rows)] + [dma((nr,))] * 4
+    elif kind == "pair":
+        scratch = [float_buffer(nb, PAD, cols), dma((nb,)), dma((nb,))]
+    else:
+        first, then = (nr, nb) if kind == "slice" else (nb, nr)
+        chunk = cols // nb
+        scratch = [float_buffer(first, PAD, chunk), float_buffer(PAD, chunk), float_buffer(PAD, size)]
+        scratch += [dma((first,))] * 2 + [dma((then,))] * 2
+    whole = pl.BlockSpec(memory_space=pltpu.VMEM)
+    return pl.pallas_call(
+        functools.partial(joint_kernel, kind, nb, nr),
+        out_shape=(
+            jax.ShapeDtypeStruct((PAD, size), jnp.float32),
+            jax.ShapeDtypeStruct((PAD, wide), jnp.float32),
+        ),
+        in_specs=[whole] * len(operands) + [pl.BlockSpec(memory_space=pl.ANY)],
+        out_specs=(whole, whole),
+        scratch_shapes=[float_buffer(rows, cols), dma] + scratch,
+        compiler_params=pltpu.CompilerParams(
+            collective_id=len(KINDS) + ("plane", "slice", "turn", "pair").index(kind),
+            has_side_effects=True,
+            vmem_limit_bytes=32 * 1024 * 1024,
+        ),
+    )(*operands, block)
+
+
 def to_low(values):
     return lax.reduce_precision(values, 8, 7).astype(jnp.bfloat16)
 
@@ -528,24 +615,24 @@
     def normal(vector):
         return jnp.sum(vector * vector, axis=1)
 
-    start = plane_sum(nb, nr, jnp.dot(targets, kmat, preferred_element_type=jnp.float32) / count_all)
-    start = factor_backward(tri_inverse, start)
-    start = turn_sum(nb, nr, start, jnp.zeros_like(start))
-    rhs = swapped("pair", nb, nr, factor_backward(aux_inverse, start))
-    first = slice_sum(nb, nr, factor_forward(aux_inverse, rhs))
-    joined = plane_sum(nb, nr, with_scalars(factor_forward(tri_inverse, first), normal(rhs)))
+    start = jnp.dot(targets, kmat, preferred_element_type=jnp.float32) / count_all
+    start = joint_sum("plane", nb, nr, tri_inverse, start)[1]
+    start = joint_sum("turn", nb, nr, aux_inverse, start, jnp.zeros_like(start))[1]
+    zeros = jnp.zeros_like(start)
+    rhs, start = joint_sum("pair", nb, nr, aux_inverse, start, zeros, zeros + 1.0)
+    first, start = joint_sum("slice", nb, nr, tri_inverse, start)
+    joined = plane_sum(nb, nr, with_scalars(start, normal(rhs)))
     norm_first = joined[PAD - 1, :PAD]
     second = clean(joined)
     image, curve = images(second)
     curve = curve + ridge_weight * normal(first)
     gram = jnp.dot(image, kmat, preferred_element_type=jnp.float32) / count_all
-    joined = plane_sum(nb, nr, with_scalars(gram, curve))
+    joined, turned = joint_sum("plane", nb, nr, tri_inverse, with_scalars(gram, curve))
     step_first = ratio(norm_first, joined[PAD - 1, :PAD])
-    third = turn_sum(nb, nr, factor_backward(tri_inverse, clean(joined)), ridge_weight * first)
-    turned = swapped("pair", nb, nr, factor_backward(aux_inverse, third))
-    residual = rhs - step_first * turned
-    first_next = slice_sum(nb, nr, factor_forward(aux_inverse, residual))
-    joined = plane_sum(nb, nr, with_scalars(factor_forward(tri_inverse, first_next), normal(residual)))
+    turned = joint_sum("turn", nb, nr, aux_inverse, turned, ridge_weight * first)[1]
+    residual, start = joint_sum("pair", nb, nr, aux_inverse, turned, rhs, zeros - step_first)
+    first_next, start = joint_sum("slice", nb, nr, tri_inverse, start)
+    joined = plane_sum(nb, nr, with_scalars(start, normal(residual)))
     norm_next = joined[PAD - 1, :PAD]
     turn_weight = ratio(norm_next, norm_first)
     first_next = first_next + turn_weight * first

time: 278 us -> 236 us (0.85)
  Pallas kernels: 227 us -> 188 us
  local copies, waits for them, and re-layouts: 7.17 us -> 13.4 us
  other arithmetic: 20.1 us -> 14.2 us
    pallas_call x16 -> x8, Pallas kernels: 159 us -> 73.2 us  [call(): pl.pallas_call(functools.partial(body, nb, nr), out_shape=jax.ShapeDtypeS...]
    pallas_call x8, Pallas kernels: 68.5 us -> 115 us  [joint_sum(): pl.pallas_call(functools.partial(joint_kernel, kind, nb, nr), out_shape=(...]
    unnamed x13 -> x23, local copies, waits for them, and re-layouts: 1.89 us -> 8.7 us
where the time goes in v1:
time: 236 us; the launch traced here: 235 us
  Pallas kernels  188 us (80%)
  matrix products  19 us (8%)
  other arithmetic  14.2 us (6%)
  local copies, waits for them, and re-layouts  13.4 us (6%)
    pallas_call x8, Pallas kernels, joint_sum(): pl.pallas_call(functools.partial(joint_kernel, kind, nb, nr), out_shape=(...  115 us
    pallas_call x8, Pallas kernels, call(): pl.pallas_call(functools.partial(body, nb, nr), out_shape=jax.ShapeDtypeS...  73.2 us
    dot_general x3, matrix products, onto_rows(): lax.dot_general(low, kmat, (((1,), (1,)), ((), ())), preferred_element_ty...  10.7 us
    unnamed x23, local copies, waits for them, and re-layouts  8.7 us

profile of v1, /device:TPU:0, one launch (start us, length us, event | category | flops | bytes accessed | tf_op | source)
XLA Modules:
  0.0 235.2 jit_solution(1550469365762645466)
XLA Ops:
  0.0 0.9 convert_reduce_fusion
  0.9 0.7 multiply_add_fusion.1
  1.6 0.7 convert_element_type.86
  2.3 1.5 pad_maximum_fusion.x_ref
  3.8 6.8 %shard_map.64 = bf16[2,272,128]{2,1,0:T(8,128)(2,1)} custom-call(bf16[272,128]{1,0:T(8,128)(2,1)} %pad_maximum_fusion.x_ref), custom_call_target="tpu_custom_call" | custom-call | tf_op jit(solution)/shard_map/pallas_call | solution.py:318
  10.6 0.9 slice.58
  11.5 0.0 slice-start
  11.5 2.0 fusion.1
  13.5 0.0 slice-start.2
  13.5 0.2 fusion.3
  13.7 0.0 slice-start.3
  13.7 0.0 slice-start.1
  13.7 3.7 %exponential_convert_fusion = bf16[512,4096]{1,0:T(8,128)(2,1)S(1)} fusion(bf16[512,128]{1,0:T(8,128)(2,1)S(1)} %bitcast.46, bf16[4096,128]{1,0:T(8,128)(2,1)} %param.9, f32[4096]{0:T(1024)S(1)} %fusion.1, f32[512]{0:T(512)S(1)} %fusion.3), kind=kOutput, calls=%fused_computation | convolution fusion | flops 549453824 | bytes 5392384 | tf_op jit(solution)/shard_map/dot_general | solution.py:582
  17.4 0.0 copy-start.2
  17.5 0.7 slice_bitcast_fusion.1
  18.2 1.1 copy-done.2
  19.4 0.7 convolution_multiply_fusion.1.refs_0_
  20.1 0.0 slice-done.2
  20.1 20.1 %shard_map.65 = (f32[8,4096]{1,0:T(8,128)}, f32[8,512]{1,0:T(8,128)S(1)}) custom-call(f32[8,4096]{1,0:T(8,128)S(1)} %convolution_multiply_fusion.1.refs_0_, f32[4096,512]{1,0:T(8,128)S(1)} %bitcast.43), custom_call_target="tpu_custom_call" | custom-call | tf_op jit(solution)/shard_map/pallas_call | solution.py:541
  40.2 14.0 %shard_map.66 = (f32[8,4096]{1,0:T(8,128)}, f32[8,512]{1,0:T(8,128)S(1)}) custom-call(f32[8,512]{1,0:T(8,128)S(1)} %get-tuple-element.18.refs_0_, f32[8,512]{1,0:T(8,128)S(1)} %broadcast_in_dim.68.refs_1_, f32[4096,512]{1,0:T(8,128)S(1)} %bitcast.41), custom_call_target="tpu_custom_call" | custom-call | tf_op jit(solution)/shard_map/pallas_call | solution.py:541
  54.2 9.6 %shard_map.67 = (f32[8,512]{1,0:T(8,128)S(1)}, f32[8,4096]{1,0:T(8,128)S(1)}) custom-call(f32[8,512]{1,0:T(8,128)S(1)} %get-tuple-element.19.refs_0_, f32[8,512]{1,0:T(8,128)S(1)} %broadcast_in_dim.68.refs_1_, f32[8,512]{1,0:T(8,128)S(1)} %broadcast_in_dim.66.refs_2_, f32[4096,512]{1,0:T(8,128)S(1)} %bitcast.41), custom_call_target="tpu_custom_call" | custom-call | tf_op jit(solution)/shard_map/pallas_call | solution.py:541
  63.8 14.6 %shard_map.68 = (f32[8,512]{1,0:T(8,128)S(1)}, f32[8,4096]{1,0:T(8,128)S(1)}) custom-call(f32[8,4096]{1,0:T(8,128)S(1)} %get-tuple-element.20.refs_0_, f32[4096,512]{1,0:T(8,128)S(1)} %bitcast.43), custom_call_target="tpu_custom_call" | custom-call | tf_op jit(solution)/shard_map/pallas_call | solution.py:541
  78.5 0.1 multiply_reduce_fusion.5
  78.6 0.7 pad_add_fusion.1.x_ref
  79.2 17.3 %shard_map.69 = f32[8,4096]{1,0:T(8,128)} custom-call(f32[8,4096]{1,0:T(8,128)} %pad_add_fusion.1.x_ref), custom_call_target="tpu_custom_call" | custom-call | tf_op jit(solution)/shard_map/pallas_call | solution.py:318
  96.5 1.0 reduce-precision_convert_fusion.6
  97.5 3.4 %fusion.6 = f32[24,512]{1,0:T(8,128)S(1)} fusion(bf16[512,4096]{1,0:T(8,128)(2,1)} %copy-done.2, bf16[8,4096]{1,0:T(8,128)(2,1)S(1)} %get-tuple-element.36, bf16[8,4096]{1,0:T(8,128)(2,1)S(1)} %get-tuple-element.37, bf16[8,4096]{1,0:T(8,128)(2,1)S(1)} %get-tuple-element.35), kind=kOutput, calls=%fused_computation.14 | convolution fusion | flops 101253120 | bytes 4440064 | tf_op jit(solution)/shard_map/dot_general | solution.py:595
  100.9 0.6 pad_maximum_fusion.1.x_ref
  101.5 5.3 %shard_map.70 = f32[16,512]{1,0:T(8,128)} custom-call(f32[16,512]{1,0:T(8,128)} %pad_maximum_fusion.1.x_ref), custom_call_target="tpu_custom_call" | custom-call | tf_op jit(solution)/shard_map/pallas_call | solution.py:318
  106.8 0.9 broadcast_multiply_fusion
  107.7 2.9 %fusion.refs_0_ = f32[8,4096]{1,0:T(8,128)S(1)} fusion(bf16[512,4096]{1,0:T(8,128)(2,1)} %copy-done.2, f32[1,8]{1,0:T(1,128)S(1)} %add_bitcast_fusion.1, f32[16,512]{1,0:T(8,128)} %shard_map.70), kind=kOutput, calls=%fused_computation.2 | convolution fusion | flops 33628160 | bytes 4341792 | tf_op jit(solution)/shard_map/dot_general | solution.py:629
  110.6 3.4 %copy-done.1 = f32[4096,512]{1,0:T(8,128)S(1)} copy-done((f32[4096,512]{1,0:T(8,128)S(1)}, f32[4096,512]{1,0:T(8,128)}, u32[]{:S(2)}) %copy-start.1) | copy-done | bytes 8388632
  114.0 17.9 %shard_map.71 = (f32[8,4096]{1,0:T(8,128)S(1)}, f32[8,512]{1,0:T(8,128)S(1)}) custom-call(f32[8,4096]{1,0:T(8,128)S(1)} %fusion.refs_0_, f32[4096,512]{1,0:T(8,128)S(1)} %copy-done.1), custom_call_target="tpu_custom_call" | custom-call | tf_op jit(solution)/shard_map/pallas_call | solution.py:541
  131.9 0.0 copy-start
  131.9 3.4 %copy-done = f32[4096,512]{1,0:T(8,128)S(1)} copy-done((f32[4096,512]{1,0:T(8,128)S(1)}, f32[4096,512]{1,0:T(8,128)}, u32[]{:S(2)}) %copy-start) | copy-done | bytes 8388632
  135.3 14.0 %shard_map.72 = (f32[8,4096]{1,0:T(8,128)}, f32[8,512]{1,0:T(8,128)S(1)}) custom-call(f32[8,512]{1,0:T(8,128)S(1)} %get-tuple-element.25.refs_0_, f32[8,512]{1,0:T(8,128)S(1)} %get-tuple-element.44.refs_1_, f32[4096,512]{1,0:T(8,128)S(1)} %copy-done), custom_call_target="tpu_custom_call" | custom-call | tf_op jit(solution)/shard_map/pallas_call | solution.py:541
  149.3 0.0 slice-start.5
  149.3 0.1 sub.27.refs_2_
  149.4 9.7 %shard_map.73 = (f32[8,512]{1,0:T(8,128)S(1)}, f32[8,4096]{1,0:T(8,128)S(1)}) custom-call(f32[8,512]{1,0:T(8,128)S(1)} %get-tuple-element.26.refs_0_, f32[8,512]{1,0:T(8,128)S(1)} %get-tuple-element.22.refs_1_, f32[8,512]{1,0:T(8,128)S(1)} %sub.27.refs_2_, f32[4096,512]{1,0:T(8,128)S(1)} %copy-done), custom_call_target="tpu_custom_call" | custom-call | tf_op jit(solution)/shard_map/pallas_call | solution.py:541
  159.1 15.0 %shard_map.74 = (f32[8,512]{1,0:T(8,128)S(1)}, f32[8,4096]{1,0:T(8,128)S(1)}) custom-call(f32[8,4096]{1,0:T(8,128)S(1)} %get-tuple-element.27.refs_0_, f32[4096,512]{1,0:T(8,128)S(1)} %bitcast.45), custom_call_target="tpu_custom_call" | custom-call | tf_op jit(solution)/shard_map/pallas_call | solution.py:541
  174.2 0.1 multiply_reduce_fusion.2
  174.3 0.7 pad_add_fusion.x_ref
  174.9 16.8 %shard_map.75 = f32[8,4096]{1,0:T(8,128)} custom-call(f32[8,4096]{1,0:T(8,128)} %pad_add_fusion.x_ref), custom_call_target="tpu_custom_call" | custom-call | tf_op jit(solution)/shard_map/pallas_call | solution.py:318
  191.8 0.7 bitcast_select_fusion
  192.4 1.0 reduce-precision_convert_fusion.3
  193.5 0.7 slice_bitcast_fusion.2
  194.1 0.1 copy.14
  194.2 0.2 multiply_reduce_fusion
  194.4 3.4 %fusion.12 = f32[24,512]{1,0:T(8,128)S(1)} fusion(bf16[512,4096]{1,0:T(8,128)(2,1)} %copy-done.2, bf16[8,4096]{1,0:T(8,128)(2,1)S(1)} %get-tuple-element.39, bf16[8,4096]{1,0:T(8,128)(2,1)S(1)} %get-tuple-element.38, bf16[8,4096]{1,0:T(8,128)(2,1)S(1)} %get-tuple-element.31), kind=kOutput, calls=%fused_computation.20 | convolution fusion | flops 101253120 | bytes 4440064 | tf_op jit(solution)/shard_map/dot_general | solution.py:595
  197.8 0.6 pad_maximum_fusion.2.x_ref
  198.5 5.3 %shard_map.76 = f32[16,512]{1,0:T(8,128)} custom-call(f32[16,512]{1,0:T(8,128)} %pad_maximum_fusion.2.x_ref), custom_call_target="tpu_custom_call" | custom-call | tf_op jit(solution)/shard_map/pallas_call | solution.py:318
  203.8 0.9 multiply_reduce_fusion.1
  204.6 0.1 copy.13
  204.7 0.6 pad.26.x_ref
  205.3 8.0 %shard_map.77 = f32[8,128]{1,0:T(8,128)} custom-call(f32[8,128]{1,0:T(8,128)} %pad.26.x_ref), custom_call_target="tpu_custom_call" | custom-call | tf_op jit(solution)/shard_map/pallas_call | solution.py:318
  213.4 0.8 select_reduce_fusion
  214.2 4.0 %fusion.18.x_ref = f32[8,512]{1,0:T(8,128)} fusion(bf16[512,4096]{1,0:T(8,128)(2,1)} %copy-done.2, f32[8,4096]{1,0:T(8,128)S(1)} %get-tuple-element.32, f32[8,4096]{1,0:T(8,128)S(1)} %copy-done.3, f32[8]{0:T(128)S(1)} %select_reduce_fusion, f32[8]{0:T(128)S(1)} %get-tuple-element.34, pred[8]{0:T(512)(128)(4,1)S(1)} %iota_compare_fusion.4), kind=kOutput, calls=%fused_computation.39 | convolution fusion | flops 33751040 | bytes 4472904 | tf_op jit(solution)/shard_map/dot_general | solution.py:595
  218.2 5.1 %shard_map.78 = f32[8,512]{1,0:T(8,128)} custom-call(f32[8,512]{1,0:T(8,128)} %fusion.18.x_ref), custom_call_target="tpu_custom_call" | custom-call | tf_op jit(solution)/shard_map/pallas_call | solution.py:318
  223.3 1.0 fusion.2
  224.3 0.1 reshape.116
  224.4 0.6 pad.27.x_ref
  225.0 8.6 %shard_map.79 = f32[16,8,128]{2,1,0:T(8,128)} custom-call(f32[16,8,128]{2,1,0:T(8,128)} %pad.27.x_ref), custom_call_target="tpu_custom_call" | custom-call | tf_op jit(solution)/shard_map/pallas_call | solution.py:318
  233.6 0.8 slice_bitcast_fusion
  234.5 0.7 reshape.117
  (28 shorter events, 0.2 us)
Async XLA Ops:
  11.5 28.6 %slice-start = ((s8[8388608]{0:T(1024)(128)(4,1)}), s8[4194304]{0:T(1024)(128)(4,1)S(1)}, s32[]{:S(2)}) async-start(s8[8388608]{0:T(1024)(128)(4,1)} %bitcast.40), calls=%async_computation | async-start | bytes 8388608
  13.5 6.5 %slice-start.2 = ((s8[8388608]{0:T(1024)(128)(4,1)}), s8[4194304]{0:T(1024)(128)(4,1)S(1)}, s32[]{:S(2)}) async-start(s8[8388608]{0:T(1024)(128)(4,1)} %bitcast.42), calls=%async_computation.2 | async-start | bytes 8388608
  13.7 6.4 %slice-start.3 = ((s8[8388608]{0:T(1024)(128)(4,1)}), s8[4194304]{0:T(1024)(128)(4,1)S(1)}, s32[]{:S(2)}) async-start(s8[8388608]{0:T(1024)(128)(4,1)} %bitcast.42), calls=%async_computation.3 | async-start | bytes 8388608
  13.7 26.5 %slice-start.1 = ((s8[8388608]{0:T(1024)(128)(4,1)}), s8[4194304]{0:T(1024)(128)(4,1)S(1)}, s32[]{:S(2)}) async-start(s8[8388608]{0:T(1024)(128)(4,1)} %bitcast.40), calls=%async_computation.1 | async-start | bytes 8388608
  17.4 1.9 copy-start.2
  110.6 3.4 %copy-start.1 = (f32[4096,512]{1,0:T(8,128)S(1)}, f32[4096,512]{1,0:T(8,128)}, u32[]{:S(2)}) copy-start(f32[4096,512]{1,0:T(8,128)} %refs_1_.7) | copy-start | bytes 25165828
  131.9 3.4 %copy-start = (f32[4096,512]{1,0:T(8,128)S(1)}, f32[4096,512]{1,0:T(8,128)}, u32[]{:S(2)}) copy-start(f32[4096,512]{1,0:T(8,128)} %refs_3_.3) | copy-start | bytes 25165828
  135.3 14.0 %copy-start.3 = (f32[8,4096]{1,0:T(8,128)S(1)}, f32[8,4096]{1,0:T(8,128)}, u32[]{:S(2)}) copy-start(f32[8,4096]{1,0:T(8,128)} %shard_map.69) | copy-start | bytes 393220
  135.3 23.8 %slice-start.4 = ((s8[8388608]{0:T(1024)(128)(4,1)}), s8[4194304]{0:T(1024)(128)(4,1)S(1)}, s32[]{:S(2)}) async-start(s8[8388608]{0:T(1024)(128)(4,1)} %bitcast.44), calls=%async_computation.4 | async-start | bytes 8388608
  149.3 9.8 %slice-start.5 = ((s8[8388608]{0:T(1024)(128)(4,1)}), s8[4194304]{0:T(1024)(128)(4,1)S(1)}, s32[]{:S(2)}) async-start(s8[8388608]{0:T(1024)(128)(4,1)} %bitcast.44), calls=%async_computation.5 | async-start | bytes 8388608

commit v2 on v1

--- a/solution.py
+++ b/solution.py
@@ -25,7 +25,7 @@
     pl.semaphore_wait(barrier, count - 1)
 
 
-def exchange(make, count, then):
+def exchange(make, count, then, meanwhile=None):
     def send(k, carry):
         make(k).start()
         return carry
@@ -39,6 +39,8 @@
         return carry
 
     lax.fori_loop(1, count, send, 0)
+    if meanwhile is not None:
+        meanwhile()
     lax.fori_loop(1, count, arrive, 0)
     if then is not None:
         then()
@@ -74,7 +76,7 @@
     return make
 
 
-def plane_kernel(nb, nr, x_ref, o_ref, land, full, s1, r1, s2, r2):
+def plane_kernel(nb, nr, x_ref, o_ref, land, full, s1, r1, s2, r2, meanwhile=None):
     b, r = lax.axis_index("blk"), lax.axis_index("rows")
     chunk = land.shape[2]
     greet(lambda k: (b, lax.rem(r + k, nr)), nr)
@@ -95,11 +97,11 @@
             device_id_type=MESH,
         )
 
-    exchange(gather, nr, None)
+    exchange(gather, nr, None, meanwhile)
     o_ref[...] = full[...]
 
 
-def slice_kernel(nb, nr, x_ref, o_ref, land, mine, full, s1, r1, s2, r2):
+def slice_kernel(nb, nr, x_ref, o_ref, land, mine, full, s1, r1, s2, r2, meanwhile):
     b, r = lax.axis_index("blk"), lax.axis_index("rows")
     me = b * nr + r
     chunk = land.shape[2]
@@ -164,6 +166,7 @@
         def _():
             full[:, spot(part, chunk)] = mine[...]
 
+    meanwhile()
     for q in range(nb):
 
         @pl.when(r * nb + q != me)
@@ -179,7 +182,7 @@
     o_ref[...] = full[...]
 
 
-def turn_kernel(nb, nr, x_ref, add_ref, o_ref, land, mine, full, s1, r1, s2, r2):
+def turn_kernel(nb, nr, x_ref, add_ref, o_ref, land, mine, full, s1, r1, s2, r2, meanwhile):
     b, r = lax.axis_index("blk"), lax.axis_index("rows")
     me = b * nr + r
     chunk = land.shape[2]
@@ -270,6 +273,7 @@
     def _():
         full[:, spot(part, chunk)] = mine[...]
 
+    meanwhile()
     lax.fori_loop(0, nr, arrive, 0)
 
     @pl.when(plane != b)
@@ -280,7 +284,7 @@
     o_ref[...] = full[...]
 
 
-def swap_kernel(kind, nb, nr, x_ref, o_ref, land, s1, r1):
+def swap_kernel(kind, nb, nr, x_ref, o_ref, land, s1, r1, meanwhile=None):
     b, r = lax.axis_index("blk"), lax.axis_index("rows")
     across = kind in ("pair", "images", "share")
     parts, own = (nb, b) if across else (nr, r)
@@ -307,7 +311,7 @@
     def finish():
         o_ref[...] = land[...] if kind in ("move", "share") else add_parts(land)
 
-    exchange(make, parts, finish)
+    exchange(make, parts, finish, meanwhile)
 
 
 KINDS = ("plane", "slice", "turn", "pair", "images", "share", "total", "move")
@@ -408,7 +412,7 @@
 def exact_product(dims, vector, block):
     stacked = jnp.concatenate(three_parts(vector), axis=0).astype(jnp.bfloat16)
     total = None
-    for part in reversed(three_parts(block)):
+    for part in reversed(block):
         product = lax.dot_general(
             stacked, part.astype(jnp.bfloat16), dims, preferred_element_type=jnp.float32
         )
@@ -418,11 +422,11 @@
 
 
 def forward_kernel(u_ref, block_ref, o_ref):
-    o_ref[...] = exact_product((((1,), (1,)), ((), ())), u_ref[...], block_ref[...])
+    o_ref[...] = exact_product((((1,), (1,)), ((), ())), u_ref[...], three_parts(block_ref[...]))
 
 
 def backward_kernel(u_ref, block_ref, o_ref):
-    product = exact_product((((1,), (0,)), ((), ())), u_ref[...], block_ref[...])
+    product = exact_product((((1,), (0,)), ((), ())), u_ref[...], three_parts(block_ref[...]))
 
     @pl.when(pl.program_id(0) == 0)
     def _():
@@ -469,11 +473,11 @@
 
 
 def factor_loop(forward, vector_ref, clean, block, p_ref):
-    steps = block.shape[0] // STEP
+    steps = block.shape[1] // STEP
     lines = lax.broadcasted_iota(jnp.int32, (PAD, STEP), 0)
 
     def visit(i, carry):
-        piece = block[spot(i, STEP), :]
+        piece = [block[index, spot(i, STEP), :] for index in range(3)]
         if forward:
             p_ref[:, spot(i, STEP)] = exact_product(
                 (((1,), (1,)), ((), ())), vector_ref[...], piece
@@ -492,21 +496,32 @@
 
 def joint_kernel(kind, nb, nr, *refs):
     inputs = {"plane": 1, "slice": 1, "turn": 2, "pair": 3}[kind]
-    block_ref, o_ref, p_ref, block, block_sem = refs[inputs : inputs + 5]
-    rest = refs[inputs + 5 :]
+    block_ref, o_ref, p_ref, block, split, block_sem = refs[inputs : inputs + 6]
+    rest = refs[inputs + 6 :]
     load = pltpu.make_async_copy(block_ref, block, block_sem)
     load.start()
+
+    def meanwhile():
+        load.wait()
+
+        def visit(i, carry):
+            piece = spot(i, STEP)
+            for index, part in enumerate(three_parts(block[piece, :])):
+                split[index, piece, :] = part.astype(jnp.bfloat16)
+            return carry
+
+        lax.fori_loop(0, block.shape[0] // STEP, visit, 0)
+
     if kind == "plane":
-        plane_kernel(nb, nr, refs[0], o_ref, *rest)
+        plane_kernel(nb, nr, refs[0], o_ref, *rest, meanwhile)
     elif kind == "slice":
-        slice_kernel(nb, nr, refs[0], o_ref, *rest)
+        slice_kernel(nb, nr, refs[0], o_ref, *rest, meanwhile)
     elif kind == "turn":
-        turn_kernel(nb, nr, refs[0], refs[1], o_ref, *rest)
+        turn_kernel(nb, nr, refs[0], refs[1], o_ref, *rest, meanwhile)
     else:
-        swap_kernel("pair", nb, nr, refs[0], o_ref, *rest)
+        swap_kernel("pair", nb, nr, refs[0], o_ref, *rest, meanwhile)
         o_ref[...] = refs[1][...] + refs[2][...] * o_ref[...]
-    load.wait()
-    factor_loop(kind in ("slice", "pair"), o_ref, kind == "plane", block, p_ref)
+    factor_loop(kind in ("slice", "pair"), o_ref, kind == "plane", split, p_ref)
 
 
 def joint_sum(kind, nb, nr, block, *operands):
@@ -544,9 +559,10 @@
             jax.ShapeDtypeStruct((PAD, size), jnp.float32),
             jax.ShapeDtypeStruct((PAD, wide), jnp.float32),
         ),
-        in_specs=[whole] * len(operands) + [pl.BlockSpec(memory_space=pl.ANY)],
+        in_specs=[whole] * len(operands) + [pl.BlockSpec(memory_space=pltpu.MemorySpace.HBM)],
         out_specs=(whole, whole),
-        scratch_shapes=[float_buffer(rows, cols), dma] + scratch,
+        scratch_shapes=[float_buffer(rows, cols), pltpu.VMEM((3, rows, cols), jnp.bfloat16), dma]
+        + scratch,
         compiler_params=pltpu.CompilerParams(
             collective_id=len(KINDS) + ("plane", "slice", "turn", "pair").index(kind),
             has_side_effects=True,

time: 236 us -> 232 us (0.983)
  Pallas kernels: 188 us -> 184 us
    pallas_call x8, Pallas kernels: 115 us -> 112 us  [joint_sum(): pl.pallas_call(functools.partial(joint_kernel, kind, nb, nr), out_shape=(...]
where the time goes in v2:
time: 232 us; the launch traced here: 231 us
  Pallas kernels  184 us (79%)
  matrix products  19 us (8%)
  other arithmetic  14.2 us (6%)
  local copies, waits for them, and re-layouts  13.4 us (6%)
    pallas_call x8, Pallas kernels, joint_sum(): pl.pallas_call(functools.partial(joint_kernel, kind, nb, nr), out_shape=(...  112 us
    pallas_call x8, Pallas kernels, call(): pl.pallas_call(functools.partial(body, nb, nr), out_shape=jax.ShapeDtypeS...  71.2 us
    dot_general x3, matrix products, onto_rows(): lax.dot_general(low, kmat, (((1,), (1,)), ((), ())), preferred_element_ty...  10.7 us
    unnamed x23, local copies, waits for them, and re-layouts  8.7 us

profile of v2, /device:TPU:0, one launch (start us, length us, event | category | flops | bytes accessed | tf_op | source)
XLA Modules:
  0.0 230.6 jit_solution(1739752326706683572)
XLA Ops:
  0.0 0.9 convert_reduce_fusion
  0.9 0.7 multiply_add_fusion.1
  1.6 0.7 convert_element_type.86
  2.3 1.5 pad_maximum_fusion.x_ref
  3.8 6.8 %shard_map.64 = bf16[2,272,128]{2,1,0:T(8,128)(2,1)} custom-call(bf16[272,128]{1,0:T(8,128)(2,1)} %pad_maximum_fusion.x_ref), custom_call_target="tpu_custom_call" | custom-call | tf_op jit(solution)/shard_map/pallas_call | solution.py:322
  10.6 0.9 slice.58
  11.5 0.0 slice-start
  11.5 2.0 fusion.1
  13.5 0.0 slice-start.2
  13.5 0.2 fusion.3
  13.7 0.0 slice-start.3
  13.7 0.0 slice-start.1
  13.7 3.7 %exponential_convert_fusion = bf16[512,4096]{1,0:T(8,128)(2,1)S(1)} fusion(bf16[512,128]{1,0:T(8,128)(2,1)S(1)} %bitcast.46, bf16[4096,128]{1,0:T(8,128)(2,1)} %param.9, f32[4096]{0:T(1024)S(1)} %fusion.1, f32[512]{0:T(512)S(1)} %fusion.3), kind=kOutput, calls=%fused_computation | convolution fusion | flops 549453824 | bytes 5392384 | tf_op jit(solution)/shard_map/dot_general | solution.py:598
  17.4 0.0 copy-start.2
  17.5 0.7 slice_bitcast_fusion.1
  18.2 1.1 copy-done.2
  19.4 0.7 convolution_multiply_fusion.1.refs_0_
  20.1 19.4 %shard_map.65 = (f32[8,4096]{1,0:T(8,128)}, f32[8,512]{1,0:T(8,128)S(1)}) custom-call(f32[8,4096]{1,0:T(8,128)S(1)} %convolution_multiply_fusion.1.refs_0_, f32[4096,512]{1,0:T(8,128)S(1)} %bitcast.43), custom_call_target="tpu_custom_call" | custom-call | tf_op jit(solution)/shard_map/pallas_call | solution.py:556
  39.5 13.2 %shard_map.66 = (f32[8,4096]{1,0:T(8,128)}, f32[8,512]{1,0:T(8,128)S(1)}) custom-call(f32[8,512]{1,0:T(8,128)S(1)} %get-tuple-element.18.refs_0_, f32[8,512]{1,0:T(8,128)S(1)} %broadcast_in_dim.68.refs_1_, f32[4096,512]{1,0:T(8,128)S(1)} %bitcast.41), custom_call_target="tpu_custom_call" | custom-call | tf_op jit(solution)/shard_map/pallas_call | solution.py:556
  52.7 9.6 %shard_map.67 = (f32[8,512]{1,0:T(8,128)S(1)}, f32[8,4096]{1,0:T(8,128)S(1)}) custom-call(f32[8,512]{1,0:T(8,128)S(1)} %get-tuple-element.19.refs_0_, f32[8,512]{1,0:T(8,128)S(1)} %broadcast_in_dim.68.refs_1_, f32[8,512]{1,0:T(8,128)S(1)} %broadcast_in_dim.66.refs_2_, f32[4096,512]{1,0:T(8,128)S(1)} %bitcast.41), custom_call_target="tpu_custom_call" | custom-call | tf_op jit(solution)/shard_map/pallas_call | solution.py:556
  62.4 14.9 %shard_map.68 = (f32[8,512]{1,0:T(8,128)S(1)}, f32[8,4096]{1,0:T(8,128)S(1)}) custom-call(f32[8,4096]{1,0:T(8,128)S(1)} %get-tuple-element.20.refs_0_, f32[4096,512]{1,0:T(8,128)S(1)} %bitcast.43), custom_call_target="tpu_custom_call" | custom-call | tf_op jit(solution)/shard_map/pallas_call | solution.py:556
  77.3 0.1 multiply_reduce_fusion.5
  77.4 0.7 pad_add_fusion.1.x_ref
  78.1 16.3 %shard_map.69 = f32[8,4096]{1,0:T(8,128)} custom-call(f32[8,4096]{1,0:T(8,128)} %pad_add_fusion.1.x_ref), custom_call_target="tpu_custom_call" | custom-call | tf_op jit(solution)/shard_map/pallas_call | solution.py:322
  94.4 1.0 reduce-precision_convert_fusion.6
  95.4 3.4 %fusion.6 = f32[24,512]{1,0:T(8,128)S(1)} fusion(bf16[512,4096]{1,0:T(8,128)(2,1)} %copy-done.2, bf16[8,4096]{1,0:T(8,128)(2,1)S(1)} %get-tuple-element.36, bf16[8,4096]{1,0:T(8,128)(2,1)S(1)} %get-tuple-element.37, bf16[8,4096]{1,0:T(8,128)(2,1)S(1)} %get-tuple-element.35), kind=kOutput, calls=%fused_computation.14 | convolution fusion | flops 101253120 | bytes 4440064 | tf_op jit(solution)/shard_map/dot_general | solution.py:611
  98.8 0.6 pad_maximum_fusion.1.x_ref
  99.4 5.3 %shard_map.70 = f32[16,512]{1,0:T(8,128)} custom-call(f32[16,512]{1,0:T(8,128)} %pad_maximum_fusion.1.x_ref), custom_call_target="tpu_custom_call" | custom-call | tf_op jit(solution)/shard_map/pallas_call | solution.py:322
  104.7 0.9 broadcast_multiply_fusion
  105.6 2.9 %fusion.refs_0_ = f32[8,4096]{1,0:T(8,128)S(1)} fusion(bf16[512,4096]{1,0:T(8,128)(2,1)} %copy-done.2, f32[1,8]{1,0:T(1,128)S(1)} %add_bitcast_fusion.1, f32[16,512]{1,0:T(8,128)} %shard_map.70), kind=kOutput, calls=%fused_computation.2 | convolution fusion | flops 33628160 | bytes 4341792 | tf_op jit(solution)/shard_map/dot_general | solution.py:645
  108.5 3.4 %copy-done.1 = f32[4096,512]{1,0:T(8,128)S(1)} copy-done((f32[4096,512]{1,0:T(8,128)S(1)}, f32[4096,512]{1,0:T(8,128)}, u32[]{:S(2)}) %copy-start.1) | copy-done | bytes 8388632
  111.9 17.1 %shard_map.71 = (f32[8,4096]{1,0:T(8,128)S(1)}, f32[8,512]{1,0:T(8,128)S(1)}) custom-call(f32[8,4096]{1,0:T(8,128)S(1)} %fusion.refs_0_, f32[4096,512]{1,0:T(8,128)S(1)} %copy-done.1), custom_call_target="tpu_custom_call" | custom-call | tf_op jit(solution)/shard_map/pallas_call | solution.py:556
  129.0 0.0 copy-start
  129.0 3.4 %copy-done = f32[4096,512]{1,0:T(8,128)S(1)} copy-done((f32[4096,512]{1,0:T(8,128)S(1)}, f32[4096,512]{1,0:T(8,128)}, u32[]{:S(2)}) %copy-start) | copy-done | bytes 8388632
  132.4 13.2 %shard_map.72 = (f32[8,4096]{1,0:T(8,128)}, f32[8,512]{1,0:T(8,128)S(1)}) custom-call(f32[8,512]{1,0:T(8,128)S(1)} %get-tuple-element.25.refs_0_, f32[8,512]{1,0:T(8,128)S(1)} %get-tuple-element.44.refs_1_, f32[4096,512]{1,0:T(8,128)S(1)} %copy-done), custom_call_target="tpu_custom_call" | custom-call | tf_op jit(solution)/shard_map/pallas_call | solution.py:556
  145.6 0.0 copy-done.3
  145.6 0.0 slice-start.5
  145.7 0.1 sub.27.refs_2_
  145.7 9.7 %shard_map.73 = (f32[8,512]{1,0:T(8,128)S(1)}, f32[8,4096]{1,0:T(8,128)S(1)}) custom-call(f32[8,512]{1,0:T(8,128)S(1)} %get-tuple-element.26.refs_0_, f32[8,512]{1,0:T(8,128)S(1)} %get-tuple-element.22.refs_1_, f32[8,512]{1,0:T(8,128)S(1)} %sub.27.refs_2_, f32[4096,512]{1,0:T(8,128)S(1)} %copy-done), custom_call_target="tpu_custom_call" | custom-call | tf_op jit(solution)/shard_map/pallas_call | solution.py:556
  155.4 15.2 %shard_map.74 = (f32[8,512]{1,0:T(8,128)S(1)}, f32[8,4096]{1,0:T(8,128)S(1)}) custom-call(f32[8,4096]{1,0:T(8,128)S(1)} %get-tuple-element.27.refs_0_, f32[4096,512]{1,0:T(8,128)S(1)} %bitcast.45), custom_call_target="tpu_custom_call" | custom-call | tf_op jit(solution)/shard_map/pallas_call | solution.py:556
  170.6 0.1 multiply_reduce_fusion.2
  170.8 0.7 pad_add_fusion.x_ref
  171.4 16.1 %shard_map.75 = f32[8,4096]{1,0:T(8,128)} custom-call(f32[8,4096]{1,0:T(8,128)} %pad_add_fusion.x_ref), custom_call_target="tpu_custom_call" | custom-call | tf_op jit(solution)/shard_map/pallas_call | solution.py:322
  187.6 0.7 bitcast_select_fusion
  188.2 1.0 reduce-precision_convert_fusion.3
  189.3 0.7 slice_bitcast_fusion.2
  189.9 0.1 copy.14
  190.0 0.2 multiply_reduce_fusion
  190.2 3.4 %fusion.12 = f32[24,512]{1,0:T(8,128)S(1)} fusion(bf16[512,4096]{1,0:T(8,128)(2,1)} %copy-done.2, bf16[8,4096]{1,0:T(8,128)(2,1)S(1)} %get-tuple-element.39, bf16[8,4096]{1,0:T(8,128)(2,1)S(1)} %get-tuple-element.38, bf16[8,4096]{1,0:T(8,128)(2,1)S(1)} %get-tuple-element.31), kind=kOutput, calls=%fused_computation.20 | convolution fusion | flops 101253120 | bytes 4440064 | tf_op jit(solution)/shard_map/dot_general | solution.py:611
  193.6 0.6 pad_maximum_fusion.2.x_ref
  194.3 5.3 %shard_map.76 = f32[16,512]{1,0:T(8,128)} custom-call(f32[16,512]{1,0:T(8,128)} %pad_maximum_fusion.2.x_ref), custom_call_target="tpu_custom_call" | custom-call | tf_op jit(solution)/shard_map/pallas_call | solution.py:322
  199.6 0.9 multiply_reduce_fusion.1
  200.4 0.1 copy.13
  200.5 0.6 pad.26.x_ref
  201.1 8.0 %shard_map.77 = f32[8,128]{1,0:T(8,128)} custom-call(f32[8,128]{1,0:T(8,128)} %pad.26.x_ref), custom_call_target="tpu_custom_call" | custom-call | tf_op jit(solution)/shard_map/pallas_call | solution.py:322
  209.2 0.8 select_reduce_fusion
  209.9 4.0 %fusion.18.x_ref = f32[8,512]{1,0:T(8,128)} fusion(bf16[512,4096]{1,0:T(8,128)(2,1)} %copy-done.2, f32[8,4096]{1,0:T(8,128)S(1)} %get-tuple-element.32, f32[8,4096]{1,0:T(8,128)S(1)} %copy-done.3, f32[8]{0:T(128)S(1)} %select_reduce_fusion, f32[8]{0:T(128)S(1)} %get-tuple-element.34, pred[8]{0:T(512)(128)(4,1)S(1)} %iota_compare_fusion.4), kind=kOutput, calls=%fused_computation.39 | convolution fusion | flops 33751040 | bytes 4472904 | tf_op jit(solution)/shard_map/dot_general | solution.py:611
  213.9 5.1 %shard_map.78 = f32[8,512]{1,0:T(8,128)} custom-call(f32[8,512]{1,0:T(8,128)} %fusion.18.x_ref), custom_call_target="tpu_custom_call" | custom-call | tf_op jit(solution)/shard_map/pallas_call | solution.py:322
  219.0 1.0 fusion.2
  220.1 0.1 reshape.116
  220.2 0.6 pad.27.x_ref
  220.8 8.2 %shard_map.79 = f32[16,8,128]{2,1,0:T(8,128)} custom-call(f32[16,8,128]{2,1,0:T(8,128)} %pad.27.x_ref), custom_call_target="tpu_custom_call" | custom-call | tf_op jit(solution)/shard_map/pallas_call | solution.py:322
  229.0 0.8 slice_bitcast_fusion
  229.9 0.7 reshape.117
  (28 shorter events, 0.2 us)
Async XLA Ops:
  11.5 27.9 %slice-start = ((s8[8388608]{0:T(1024)(128)(4,1)}), s8[4194304]{0:T(1024)(128)(4,1)S(1)}, s32[]{:S(2)}) async-start(s8[8388608]{0:T(1024)(128)(4,1)} %bitcast.40), calls=%async_computation | async-start | bytes 8388608
  13.5 6.5 %slice-start.2 = ((s8[8388608]{0:T(1024)(128)(4,1)}), s8[4194304]{0:T(1024)(128)(4,1)S(1)}, s32[]{:S(2)}) async-start(s8[8388608]{0:T(1024)(128)(4,1)} %bitcast.42), calls=%async_computation.2 | async-start | bytes 8388608
  13.7 6.4 %slice-start.3 = ((s8[8388608]{0:T(1024)(128)(4,1)}), s8[4194304]{0:T(1024)(128)(4,1)S(1)}, s32[]{:S(2)}) async-start(s8[8388608]{0:T(1024)(128)(4,1)} %bitcast.42), calls=%async_computation.3 | async-start | bytes 8388608
  13.7 25.8 %slice-start.1 = ((s8[8388608]{0:T(1024)(128)(4,1)}), s8[4194304]{0:T(1024)(128)(4,1)S(1)}, s32[]{:S(2)}) async-start(s8[8388608]{0:T(1024)(128)(4,1)} %bitcast.40), calls=%async_computation.1 | async-start | bytes 8388608
  17.4 1.9 copy-start.2
  108.5 3.4 %copy-start.1 = (f32[4096,512]{1,0:T(8,128)S(1)}, f32[4096,512]{1,0:T(8,128)}, u32[]{:S(2)}) copy-start(f32[4096,512]{1,0:T(8,128)} %refs_1_.7) | copy-start | bytes 25165828
  129.0 3.4 %copy-start = (f32[4096,512]{1,0:T(8,128)S(1)}, f32[4096,512]{1,0:T(8,128)}, u32[]{:S(2)}) copy-start(f32[4096,512]{1,0:T(8,128)} %refs_3_.3) | copy-start | bytes 25165828
  132.4 13.2 %copy-start.3 = (f32[8,4096]{1,0:T(8,128)S(1)}, f32[8,4096]{1,0:T(8,128)}, u32[]{:S(2)}) copy-start(f32[8,4096]{1,0:T(8,128)} %shard_map.69) | copy-start | bytes 393220
  132.4 23.0 %slice-start.4 = ((s8[8388608]{0:T(1024)(128)(4,1)}), s8[4194304]{0:T(1024)(128)(4,1)S(1)}, s32[]{:S(2)}) async-start(s8[8388608]{0:T(1024)(128)(4,1)} %bitcast.44), calls=%async_computation.4 | async-start | bytes 8388608
  145.6 9.8 %slice-start.5 = ((s8[8388608]{0:T(1024)(128)(4,1)}), s8[4194304]{0:T(1024)(128)(4,1)S(1)}, s32[]{:S(2)}) async-start(s8[8388608]{0:T(1024)(128)(4,1)} %bitcast.44), calls=%async_computation.5 | async-start | bytes 8388608
